TPU v7x, 512 devices: a whole 4x4x16 slice. The times are simulated.
512 devices in a mesh: seq: 128 (over y, z, core), head: 4 (over x).
Axes of the slice: x: 4, y: 4, z: 16, core: 2. Of those that a mesh axis runs over, the one named last changes fastest.
Arguments:
- queries: bfloat16 [65536, 2048], P('seq', 'head'), may hold values from -6 to 6
- key_vectors: bfloat16 [65536, 2048], P('seq', 'head'), may hold values from -6 to 6
- values: bfloat16 [65536, 2048], P('seq', 'head'), may hold values from -6 to 6
- out_weight: bfloat16 [2048, 2048], P('head', 'seq'), may hold values from -4 to 4
Outputs:
- mixed: bfloat16 [65536, 2048], P('seq', 'head')
All inputs are finite; a program needn't handle non-finite values.
Results may differ from a plain program's by a relative error of at most 0.0095.
Values may be sent and summed in bfloat16 or wider, within the bound.
No kernel may reach another device: no remote copies, remote signals or barrier semaphores. Data moves between devices by JAX's collectives and lax.ppermute only.
A program may use at most 64 MiB of HBM per device.

v0:
```python
import math
import jax
import jax.numpy as jnp
from jax import lax
from jax.sharding import PartitionSpec as P

HEAD_DIM = 128
BLOCK = 128
LEVELS = 5


def partner(value, axis, stride):
    mask = 2**stride
    pairs = [(source, source ^ mask) for source in range(lax.axis_size(axis))]
    return lax.ppermute(value, axis, pairs)


def pool_mean(array_in):
    paired = array_in.astype(jnp.float32).reshape(array_in.shape[0] // 2, 2, array_in.shape[1])
    return ((paired[:, 0] + paired[:, 1]) * 0.5).astype(jnp.bfloat16)


def pool_sum(array_in):
    paired = array_in.astype(jnp.float32).reshape(array_in.shape[0] // 2, 2, array_in.shape[1])
    return (paired[:, 0] + paired[:, 1]).astype(jnp.bfloat16)


def to_blocks(array_in, head_count, block_rows):
    return array_in.reshape(-1, block_rows, head_count, array_in.shape[1] // head_count)


def swap_pairs(blocked):
    block_count = blocked.shape[0]
    return blocked.reshape((block_count // 2, 2) + blocked.shape[1:])[:, ::-1].reshape(
        blocked.shape
    )


def level_terms(
    blocked_query_rows, blocked_key_rows, blocked_value_rows, weight, logit_scale_factor
):
    attention_logits = (
        jnp.einsum(
            "bqhd,bkhd->bhqk",
            blocked_query_rows,
            blocked_key_rows,
            preferred_element_type=jnp.float32,
        )
        * logit_scale_factor
    )
    peak_score = jnp.max(attention_logits, axis=-1)
    expo = jnp.exp(attention_logits - peak_score[..., None])
    mass = weight * jnp.sum(expo, axis=-1)
    weighted_value_sum = jnp.einsum(
        "bhqk,bkhd->bqhd",
        expo.astype(jnp.bfloat16),
        blocked_value_rows,
        preferred_element_type=jnp.float32,
    )
    head_count = blocked_query_rows.shape[2]
    peak_rows = jnp.transpose(peak_score, (0, 2, 1)).reshape(-1, head_count)
    mass_rows = jnp.transpose(mass, (0, 2, 1)).reshape(-1, head_count)
    return (
        peak_rows,
        mass_rows,
        weighted_value_sum.reshape(-1, head_count, weighted_value_sum.shape[3]),
    )


def merge_level(running, terms, factor):
    running_max, running_sum, running_out = running
    peak_rows = jnp.repeat(terms[0], factor, axis=0)
    mass_rows = jnp.repeat(terms[1], factor, axis=0)
    weighted_value_sum = jnp.repeat(terms[2], factor, axis=0)
    newest = jnp.maximum(running_max, peak_rows)
    keep_old = jnp.exp(running_max - newest)
    keep_new = jnp.exp(peak_rows - newest)
    return (
        newest,
        running_sum * keep_old + mass_rows * keep_new,
        running_out * keep_old[..., None] + weighted_value_sum * keep_new[..., None],
    )


def body(queries, key_vectors, values, out_weight):
    row_count, col_count = queries.shape
    head_count = col_count // HEAD_DIM
    logit_scale_factor = 1.0 / math.sqrt(HEAD_DIM)
    seq_index = lax.axis_index("seq")
    blocked_key_rows = to_blocks(key_vectors, head_count, BLOCK)
    blocked_value_rows = to_blocks(values, head_count, BLOCK)
    near_keys = jnp.concatenate([blocked_key_rows, swap_pairs(blocked_key_rows)], axis=1)
    near_values = jnp.concatenate([blocked_value_rows, swap_pairs(blocked_value_rows)], axis=1)
    running = level_terms(
        to_blocks(queries, head_count, BLOCK), near_keys, near_values, 1.0, logit_scale_factor
    )
    level_queries, level_keys, level_values = (queries, key_vectors, values)
    far_keys, far_values = (key_vectors, values)
    is_local = True
    partner_bit = 0
    for coarse_level in range(1, LEVELS + 1):
        level_queries = pool_mean(level_queries)
        if is_local:
            level_keys = pool_mean(level_keys)
            level_values = pool_sum(level_values)
            is_local = level_keys.shape[0] >= 2 * BLOCK
        else:
            leading = seq_index >> partner_bit - 1 & 1 == 0
            level_keys = pool_mean(
                jnp.concatenate(
                    [
                        jnp.where(leading, level_keys, far_keys),
                        jnp.where(leading, far_keys, level_keys),
                    ],
                    axis=0,
                )
            )
            level_values = pool_sum(
                jnp.concatenate(
                    [
                        jnp.where(leading, level_values, far_values),
                        jnp.where(leading, far_values, level_values),
                    ],
                    axis=0,
                )
            )
        if is_local:
            blocked_key_rows = swap_pairs(to_blocks(level_keys, head_count, BLOCK))
            blocked_value_rows = swap_pairs(to_blocks(level_values, head_count, BLOCK))
        else:
            far_keys, far_values = partner((level_keys, level_values), "seq", partner_bit)
            partner_bit += 1
            blocked_key_rows = to_blocks(far_keys, head_count, BLOCK)
            blocked_value_rows = to_blocks(far_values, head_count, BLOCK)
        blocked_query_rows = to_blocks(
            level_queries, head_count, level_queries.shape[0] // blocked_key_rows.shape[0]
        )
        terms = level_terms(
            blocked_query_rows,
            blocked_key_rows,
            blocked_value_rows,
            2.0**coarse_level,
            logit_scale_factor,
        )
        running = merge_level(running, terms, 2**coarse_level)
    attended = (
        (running[2] / running[1][..., None]).reshape(row_count, col_count).astype(jnp.bfloat16)
    )
    partial_terms = jnp.dot(
        attended,
        lax.all_gather(out_weight, "seq", axis=1, tiled=True),
        preferred_element_type=jnp.float32,
    )
    rounded_terms = partial_terms.astype(jnp.bfloat16).astype(jnp.float32)
    mixed = lax.psum_scatter(
        rounded_terms.astype(jnp.bfloat16), "head", scatter_dimension=1, tiled=True
    )
    return mixed


def solution(mesh):
    in_specs = (P("seq", "head"), P("seq", "head"), P("seq", "head"), P("head", "seq"))
    out_specs = P("seq", "head")
    return jax.shard_map(body, mesh=mesh, in_specs=in_specs, out_specs=out_specs, check_vma=False)
```

profile of v0, /device:TPU:1, one launch (start us, length us, event | category | flops | bytes accessed | tf_op | source)
XLA Modules:
  0.0 223.5 jit_solution(2739491692825542733)
XLA Ops:
  7.3 1.7 reshape.785
  10.7 8.7 %collective-permute-start = (bf16[128,512]{1,0:T(8,128)(2,1)S(1)}, bf16[128,512]{1,0:T(8,128)(2,1)}, u32[]{:S(2)}, u32[]{:S(2)}) collective-permute-start(bf16[128,512]{1,0:T(8,128)(2,1)S(1)} %fusion.53), channel_id=1, source_target_pairs={{0,4},{4,0},{8,12},{12,8},{16,20},{20,16},{24,28},{28,24},{32,36},... | collective-permute-start | bytes 393224 | tf_op jit(solution)/shard_map/ppermute | solution.py:15
  22.6 2.2 collective-permute-start.1
  33.2 1.0 copy.283
  35.3 1.1 convert_reduce_fusion.1
  48.4 1.7 broadcast_select_fusion.9
  51.0 1.9 collective-permute-start.3
  54.6 3.6 %collective-permute-start.2 = (bf16[128,512]{1,0:T(8,128)(2,1)S(1)}, bf16[128,512]{1,0:T(8,128)(2,1)}, u32[]{:S(2)}, u32[]{:S(2)}) collective-permute-start(bf16[128,512]{1,0:T(8,128)(2,1)S(1)} %fusion.54), channel_id=1, source_target_pairs={{0,8},{4,12},{8,0},{12,4},{16,24},{20,28},{24,16},{28,20},{32,40},... | collective-permute-start | bytes 393224 | tf_op jit(solution)/shard_map/ppermute | solution.py:15
  59.1 1.9 collective-permute-start.5
  62.3 1.1 fusion.115
  67.5 4.0 %collective-permute-start.4 = (bf16[128,512]{1,0:T(8,128)(2,1)S(1)}, bf16[128,512]{1,0:T(8,128)(2,1)}, u32[]{:S(2)}, u32[]{:S(2)}) collective-permute-start(bf16[128,512]{1,0:T(8,128)(2,1)S(1)} %fusion.55), channel_id=1, source_target_pairs={{0,16},{4,20},{8,24},{12,28},{16,0},{20,4},{24,8},{28,12},{32,48},... | collective-permute-start | bytes 393224 | tf_op jit(solution)/shard_map/ppermute | solution.py:15
  71.5 1.3 fusion.99
  75.1 5.7 %collective-permute-start.7 = (bf16[128,512]{1,0:T(8,128)(2,1)}, bf16[128,512]{1,0:T(8,128)(2,1)}, u32[]{:S(2)}, u32[]{:S(2)}) collective-permute-start(bf16[128,512]{1,0:T(8,128)(2,1)} %bitcast.335), channel_id=1, source_target_pairs={{0,32},{4,36},{8,40},{12,44},{16,48},{20,52},{24,56},{28,60},{32,0... | collective-permute-start | bytes 393224 | tf_op jit(solution)/shard_map/ppermute | solution.py:15
  81.8 1.0 copy.335
  87.5 3.5 %collective-permute-start.6 = (bf16[128,512]{1,0:T(8,128)(2,1)S(1)}, bf16[128,512]{1,0:T(8,128)(2,1)S(1)}, u32[]{:S(2)}, u32[]{:S(2)}) collective-permute-start(bf16[128,512]{1,0:T(8,128)(2,1)S(1)} %fusion.56), channel_id=1, source_target_pairs={{0,32},{4,36},{8,40},{12,44},{16,48},{20,52},{24,56},{28,60},{32,0... | collective-permute-start | bytes 393224 | tf_op jit(solution)/shard_map/ppermute | solution.py:15
  91.4 3.5 %collective-permute-done.7 = bf16[128,512]{1,0:T(8,128)(2,1)} collective-permute-done((bf16[128,512]{1,0:T(8,128)(2,1)}, bf16[128,512]{1,0:T(8,128)(2,1)}, u32[]{:S(2)}, u32[]{:S(2)}) %collective-permute-start.7) | collective-permute-done | bytes 131104 | tf_op jit(solution)/shard_map/ppermute | solution.py:15
  95.9 11.2 %collective-permute-done.6 = bf16[128,512]{1,0:T(8,128)(2,1)S(1)} collective-permute-done((bf16[128,512]{1,0:T(8,128)(2,1)S(1)}, bf16[128,512]{1,0:T(8,128)(2,1)S(1)}, u32[]{:S(2)}, u32[]{:S(2)}) %collective-permute-start.6) | collective-permute-done | bytes 131104 | tf_op jit(solution)/shard_map/ppermute | solution.py:15
  111.2 1.6 copy.297
  112.8 1.6 copy.314
  114.3 1.6 copy.326
  117.6 53.3 %all-gather.2.cloned.1.call-done = bf16[512,2048]{0,1:T(8,128)(2,1)} async-done(((bf16[512,16]{0,1:T(8,128)(2,1)}), bf16[512,2048]{0,1:T(8,128)(2,1)}) %all-gather.2.cloned.1.call-update) | async-done | bytes 2097168 | tf_op jit(solution)/shard_map/all_gather | solution.py:151
  171.1 1.6 mul.426
  179.8 3.5 %convolution_convert_fusion = bf16[512,2048]{1,0:T(8,128)(2,1)} fusion(bf16[512,2048]{0,1:T(8,128)(2,1)S(1)} %copy-done.2, f32[64,8,4,128]{3,2,1,0:T(4,128)S(1)} %bitcast.346, f32[64,8,4,128]{3,2,1,0:T(4,128)S(1)} %bitcast.341, f32[64,8,4,128]{3,2,1,0:T(4,128)S(1)} %bitcast.351, f32[64,8,4,128]{3,2,1,0:T(4,128)S(1)} %bitcast.336, ...), kind=kOutput, calls=%fused_computation | convolution fusion | flops 1079246848 | bytes 21102592 | tf_op jit(solution)/shard_map/dot_general | solution.py:149
  183.4 33.3 %reduce-scatter.2.cloned.1.call-done = bf16[512,512]{1,0:T(8,128)(2,1)} async-done(((bf16[512,2048]{1,0:T(8,128)(2,1)}), bf16[512,512]{1,0:T(8,128)(2,1)}) %reduce-scatter.2.cloned.1.call-update) | async-done | bytes 524304 | tf_op jit(solution)/shard_map/reduce_scatter | solution.py:155
  (223 shorter events, 57.1 us)
Async XLA Ops:
  6.5 164.4 %all-gather.2.cloned.1.call-start = ((), (), s32[]{:S(2)}) async-start(), calls=%async_computation.1 | async-start | bytes 2113536 | tf_op jit(solution)/shard_map/all_gather | solution.py:151
  7.3 209.4 %reduce-scatter.2.cloned.1.call-start = ((), (), s32[]{:S(2)}) async-start(), calls=%async_computation.2 | async-start | bytes 2621440 | tf_op jit(solution)/shard_map/reduce_scatter | solution.py:155
  9.8 9.7 %copy-start.1 = (bf16[512,512]{1,0:T(8,128)(2,1)S(1)}, bf16[512,512]{1,0:T(8,128)(2,1)}, u32[]{:S(2)}) copy-start(bf16[512,512]{1,0:T(8,128)(2,1)} %param.6) | copy-start | bytes 1572868
  10.7 33.1 %collective-permute-start = (bf16[128,512]{1,0:T(8,128)(2,1)S(1)}, bf16[128,512]{1,0:T(8,128)(2,1)}, u32[]{:S(2)}, u32[]{:S(2)}) collective-permute-start(bf16[128,512]{1,0:T(8,128)(2,1)S(1)} %fusion.53), channel_id=1, source_target_pairs={{0,4},{4,0},{8,12},{12,8},{16,20},{20,16},{24,28},{28,24},{32,36},... | collective-permute-start | bytes 393224 | tf_op jit(solution)/shard_map/ppermute | solution.py:15
  22.6 24.5 %collective-permute-start.1 = (bf16[128,512]{1,0:T(8,128)(2,1)}, bf16[128,512]{1,0:T(8,128)(2,1)}, u32[]{:S(2)}, u32[]{:S(2)}) collective-permute-start(bf16[128,512]{1,0:T(8,128)(2,1)} %fusion.50), channel_id=1, source_target_pairs={{0,4},{4,0},{8,12},{12,8},{16,20},{20,16},{24,28},{28,24},{32,36},... | collective-permute-start | bytes 393224 | tf_op jit(solution)/shard_map/ppermute | solution.py:15
  51.0 7.3 %collective-permute-start.3 = (bf16[128,512]{1,0:T(8,128)(2,1)S(1)}, bf16[128,512]{1,0:T(8,128)(2,1)S(1)}, u32[]{:S(2)}, u32[]{:S(2)}) collective-permute-start(bf16[128,512]{1,0:T(8,128)(2,1)S(1)} %fusion.51), channel_id=1, source_target_pairs={{0,8},{4,12},{8,0},{12,4},{16,24},{20,28},{24,16},{28,20},{32,40},... | collective-permute-start | bytes 393224 | tf_op jit(solution)/shard_map/ppermute | solution.py:15
  54.6 6.6 %collective-permute-start.2 = (bf16[128,512]{1,0:T(8,128)(2,1)S(1)}, bf16[128,512]{1,0:T(8,128)(2,1)}, u32[]{:S(2)}, u32[]{:S(2)}) collective-permute-start(bf16[128,512]{1,0:T(8,128)(2,1)S(1)} %fusion.54), channel_id=1, source_target_pairs={{0,8},{4,12},{8,0},{12,4},{16,24},{20,28},{24,16},{28,20},{32,40},... | collective-permute-start | bytes 393224 | tf_op jit(solution)/shard_map/ppermute | solution.py:15
  59.1 13.7 %collective-permute-start.5 = (bf16[128,512]{1,0:T(8,128)(2,1)S(1)}, bf16[128,512]{1,0:T(8,128)(2,1)}, u32[]{:S(2)}, u32[]{:S(2)}) collective-permute-start(bf16[128,512]{1,0:T(8,128)(2,1)S(1)} %fusion.52), channel_id=1, source_target_pairs={{0,16},{4,20},{8,24},{12,28},{16,0},{20,4},{24,8},{28,12},{32,48},... | collective-permute-start | bytes 393224 | tf_op jit(solution)/shard_map/ppermute | solution.py:15
  67.5 14.4 %collective-permute-start.4 = (bf16[128,512]{1,0:T(8,128)(2,1)S(1)}, bf16[128,512]{1,0:T(8,128)(2,1)}, u32[]{:S(2)}, u32[]{:S(2)}) collective-permute-start(bf16[128,512]{1,0:T(8,128)(2,1)S(1)} %fusion.55), channel_id=1, source_target_pairs={{0,16},{4,20},{8,24},{12,28},{16,0},{20,4},{24,8},{28,12},{32,48},... | collective-permute-start | bytes 393224 | tf_op jit(solution)/shard_map/ppermute | solution.py:15
  75.1 19.7 %collective-permute-start.7 = (bf16[128,512]{1,0:T(8,128)(2,1)}, bf16[128,512]{1,0:T(8,128)(2,1)}, u32[]{:S(2)}, u32[]{:S(2)}) collective-permute-start(bf16[128,512]{1,0:T(8,128)(2,1)} %bitcast.335), channel_id=1, source_target_pairs={{0,32},{4,36},{8,40},{12,44},{16,48},{20,52},{24,56},{28,60},{32,0... | collective-permute-start | bytes 393224 | tf_op jit(solution)/shard_map/ppermute | solution.py:15
  86.5 20.7 %copy-start.20 = (bf16[16,512]{1,0:T(8,128)(2,1)S(1)}, bf16[16,512]{1,0:T(8,128)(2,1)}, u32[]{:S(2)}) copy-start(bf16[16,512]{1,0:T(8,128)(2,1)} %convert_reduce_fusion.4) | copy-start | bytes 49156
  86.6 4.4 %copy-start.23 = (f32[4,32]{1,0:T(4,128)S(1)}, f32[4,32]{1,0:T(4,128)}, u32[]{:S(2)}) copy-start(f32[4,32]{1,0:T(4,128)} %copy-done.22) | copy-start | bytes 1540
  86.6 22.2 %copy-start.18 = (f32[512,4]{0,1:T(4,128)S(1)}, f32[512,4]{0,1:T(4,128)}, u32[]{:S(2)}) copy-start(f32[512,4]{0,1:T(4,128)} %reshape.749) | copy-start | bytes 24580
  86.6 22.2 %copy-start.19 = (f32[512,4]{0,1:T(4,128)S(1)}, f32[512,4]{0,1:T(4,128)}, u32[]{:S(2)}) copy-start(f32[512,4]{0,1:T(4,128)} %reshape.755) | copy-start | bytes 24580
  86.6 22.2 %copy-start.21 = (f32[4,4,128]{2,1,0:T(4,128)S(1)}, f32[4,4,128]{2,1,0:T(4,128)}, u32[]{:S(2)}) copy-start(f32[4,4,128]{2,1,0:T(4,128)} %fusion.1) | copy-start | bytes 24580
  86.6 22.2 %copy-start.24 = (f32[512,4]{0,1:T(4,128)S(1)}, f32[512,4]{0,1:T(4,128)}, u32[]{:S(2)}) copy-start(f32[512,4]{0,1:T(4,128)} %copy.356) | copy-start | bytes 24580
  86.6 22.2 %copy-start.25 = (f32[512,4]{0,1:T(4,128)S(1)}, f32[512,4]{0,1:T(4,128)}, u32[]{:S(2)}) copy-start(f32[512,4]{0,1:T(4,128)} %reshape.775) | copy-start | bytes 24580
  87.0 21.9 %copy-start.26 = (f32[512,4]{0,1:T(4,128)S(1)}, f32[512,4]{0,1:T(4,128)}, u32[]{:S(2)}) copy-start(f32[512,4]{0,1:T(4,128)} %reshape.777) | copy-start | bytes 24580
  87.0 21.9 %copy-start.27 = (f32[512,4]{0,1:T(4,128)S(1)}, f32[512,4]{0,1:T(4,128)}, u32[]{:S(2)}) copy-start(f32[512,4]{0,1:T(4,128)} %reshape.761) | copy-start | bytes 24580
  87.0 21.9 %copy-start.30 = (f32[512,4]{0,1:T(4,128)S(1)}, f32[512,4]{0,1:T(4,128)}, u32[]{:S(2)}) copy-start(f32[512,4]{0,1:T(4,128)} %get-tuple-element.18) | copy-start | bytes 24580
  87.0 21.9 %copy-start.31 = (f32[512,4]{0,1:T(4,128)S(1)}, f32[512,4]{0,1:T(4,128)}, u32[]{:S(2)}) copy-start(f32[512,4]{0,1:T(4,128)} %get-tuple-element.19) | copy-start | bytes 24580
  87.5 19.6 %collective-permute-start.6 = (bf16[128,512]{1,0:T(8,128)(2,1)S(1)}, bf16[128,512]{1,0:T(8,128)(2,1)S(1)}, u32[]{:S(2)}, u32[]{:S(2)}) collective-permute-start(bf16[128,512]{1,0:T(8,128)(2,1)S(1)} %fusion.56), channel_id=1, source_target_pairs={{0,32},{4,36},{8,40},{12,44},{16,48},{20,52},{24,56},{28,60},{32,0... | collective-permute-start | bytes 393224 | tf_op jit(solution)/shard_map/ppermute | solution.py:15
  109.6 6.3 %copy-start.29 = (f32[512,4]{0,1:T(4,128)S(1)}, f32[512,4]{0,1:T(4,128)}, u32[]{:S(2)}) copy-start(f32[512,4]{0,1:T(4,128)} %get-tuple-element.14) | copy-start | bytes 24580
  109.6 7.2 %copy-start.28 = (f32[512,4]{0,1:T(4,128)S(1)}, f32[512,4]{0,1:T(4,128)}, u32[]{:S(2)}) copy-start(f32[512,4]{0,1:T(4,128)} %get-tuple-element.15) | copy-start | bytes 24580
  (18 other events, 41.8 us)
Sparse Core Ops, SparseCore 0:
  10.5 160.4 all-gather.1
  183.5 33.1 reduce-scatter.1
where the time goes:
time: 224 us; the launch traced here: 223 us
  waiting for transfers between devices  102 us (46%)
  local copies, waits for them, and re-layouts  52.1 us (23%)
  starting transfers between devices  31.7 us (14%)
  between operations  14.6 us (7%)
  other arithmetic  14.2 us (6%)
  matrix products  8.56 us (4%)
    all_gather x1, waiting for transfers between devices, body(): lax.all_gather(out_weight, 'seq', axis=1, tiled=True)  53.3 us
    reduce_scatter x1, waiting for transfers between devices, body(): lax.psum_scatter(rounded_terms.astype(jnp.bfloat16), 'head', scatter_dime...  33.3 us
    ppermute x8, starting transfers between devices, partner(): return lax.ppermute(value, axis, pairs)  31.6 us
    ppermute x8, waiting for transfers between devices, partner(): return lax.ppermute(value, axis, pairs)  15 us
    exp x5, local copies, waits for them, and re-layouts, merge_level(): keep_old = jnp.exp(running_max - newest)  6.4 us
    ppermute x8, local copies, waits for them, and re-layouts, partner(): return lax.ppermute(value, axis, pairs)  6.36 us
  transfers between devices with their start and end apart: 10, of which 5 were waited for; matrix products, arithmetic and copies ran while one was open for 28% of the time, Pallas kernels for 0%

commit v1 on v0

--- a/solution.py
+++ b/solution.py
@@ -7,6 +7,13 @@
 HEAD_DIM = 128
 BLOCK = 128
 LEVELS = 5
+
+
+def _edit_inputs(work_x, net_axis):
+    b_now = jnp.concatenate(
+        lax.all_to_all(jnp.stack(lax.axis_size(net_axis) * [work_x]), net_axis, 0, 0), axis=1
+    )
+    return b_now
 
 
 def partner(value, axis, stride):
@@ -147,9 +154,7 @@
         (running[2] / running[1][..., None]).reshape(row_count, col_count).astype(jnp.bfloat16)
     )
     partial_terms = jnp.dot(
-        attended,
-        lax.all_gather(out_weight, "seq", axis=1, tiled=True),
-        preferred_element_type=jnp.float32,
+        attended, _edit_inputs(out_weight, "seq"), preferred_element_type=jnp.float32
     )
     rounded_terms = partial_terms.astype(jnp.bfloat16).astype(jnp.float32)
     mixed = lax.psum_scatter(

time: 224 us -> 238 us (1.062)
  starting transfers between devices: 31.7 us -> 48.6 us
  local copies, waits for them, and re-layouts: 52.1 us -> 35.9 us
  waiting for transfers between devices: 102 us -> 113 us
    ppermute x8, waiting for transfers between devices: 15 us -> 74.8 us  [partner(): return lax.ppermute(value, axis, pairs)]
    all_gather x1 -> x0, waiting for transfers between devices: 53.3 us -> none  [body(): lax.all_gather(out_weight, 'seq', axis=1, tiled=True)]
    all_to_all x0 -> x1, starting transfers between devices: none -> 14.8 us  [_edit_inputs(): lax.all_to_all(jnp.stack(lax.axis_size(net_axis) * [work_x]), net_axis, 0...]
    exp x10 -> x0, local copies, waits for them, and re-layouts: 7.84 us -> none  [the longest x5 6.4 us: merge_level(): keep_old = jnp.exp(running_max - newest)]
    mul x10 -> x0, local copies, waits for them, and re-layouts: 7.01 us -> none  [the longest x5 3.99 us: merge_level(): running_out * keep_old[..., None] + weighted_value_sum * keep_new[..., None]]
    reduce_scatter x1, waiting for transfers between devices: 33.3 us -> 38.4 us  [body(): lax.psum_scatter(rounded_terms.astype(jnp.bfloat16), 'head', scatter_dime...]
    convert_element_type x0 -> x1, other arithmetic: none -> 3.77 us  [body(): (running[2] / running[1][..., None]).reshape(row_count, col_count)]
  transfers between devices with their start and end apart: 10 -> 10, of which waited for: 5 -> 3; matrix products, arithmetic and copies ran while one was open for 28% -> 22% of each run, Pallas kernels for 0% -> 0%
where the time goes in v1:
time: 238 us; the launch traced here: 237 us
  waiting for transfers between devices  113 us (47%)
  starting transfers between devices  48.6 us (20%)
  local copies, waits for them, and re-layouts  35.9 us (15%)
  other arithmetic  16.4 us (7%)
  between operations  14.5 us (6%)
  matrix products  8.55 us (4%)
    ppermute x8, waiting for transfers between devices, partner(): return lax.ppermute(value, axis, pairs)  74.8 us
    reduce_scatter x1, waiting for transfers between devices, body(): lax.psum_scatter(rounded_terms.astype(jnp.bfloat16), 'head', scatter_dime...  38.4 us
    ppermute x8, starting transfers between devices, partner(): return lax.ppermute(value, axis, pairs)  33.6 us
    all_to_all x1, starting transfers between devices, _edit_inputs(): lax.all_to_all(jnp.stack(lax.axis_size(net_axis) * [work_x]), net_axis, 0...  14.8 us
    ppermute x8, local copies, waits for them, and re-layouts, partner(): return lax.ppermute(value, axis, pairs)  6.36 us
  transfers between devices with their start and end apart: 10, of which 3 were waited for; matrix products, arithmetic and copies ran while one was open for 22% of the time, Pallas kernels for 0%

profile of v1, /device:TPU:1, one launch (start us, length us, event | category | flops | bytes accessed | tf_op | source)
XLA Modules:
  0.0 237.3 jit_solution(6546082479456384387)
XLA Ops:
  6.5 1.7 reshape.874
  10.0 8.7 %collective-permute-start = (bf16[128,512]{1,0:T(8,128)(2,1)S(1)}, bf16[128,512]{1,0:T(8,128)(2,1)}, u32[]{:S(2)}, u32[]{:S(2)}) collective-permute-start(bf16[128,512]{1,0:T(8,128)(2,1)S(1)} %fusion.57), channel_id=1, source_target_pairs={{0,4},{4,0},{8,12},{12,8},{16,20},{20,16},{24,28},{28,24},{32,36},... | collective-permute-start | bytes 393224 | tf_op jit(solution)/shard_map/ppermute | solution.py:22
  21.8 1.9 collective-permute-start.1
  23.7 1.6 stack.2
  25.3 14.8 %all-to-all-start = ((bf16[128,512,16]{1,2,0:T(8,128)(2,1)}), bf16[128,512,16]{1,2,0:T(8,128)(2,1)}, u32[]{:S(2)}, u32[]{:S(2)}) async-start(bf16[128,512,16]{1,2,0:T(8,128)(2,1)} %stack.2), calls=%async_computation | async-start | bytes 4194304 | tf_op jit(solution)/shard_map/all_to_all | solution.py:14
  50.5 1.1 convert_reduce_fusion.1
  58.5 1.0 copy.252
  63.0 1.7 broadcast_select_fusion.9
  65.6 3.3 %collective-permute-start.3 = (bf16[128,512]{1,0:T(8,128)(2,1)S(1)}, bf16[128,512]{1,0:T(8,128)(2,1)S(1)}, u32[]{:S(2)}, u32[]{:S(2)}) collective-permute-start(bf16[128,512]{1,0:T(8,128)(2,1)S(1)} %fusion.55), channel_id=1, source_target_pairs={{0,8},{4,12},{8,0},{12,4},{16,24},{20,28},{24,16},{28,20},{32,40},... | collective-permute-start | bytes 393224 | tf_op jit(solution)/shard_map/ppermute | solution.py:22
  70.6 2.0 collective-permute-start.2
  72.6 60.6 %collective-permute-done.3 = bf16[128,512]{1,0:T(8,128)(2,1)S(1)} collective-permute-done((bf16[128,512]{1,0:T(8,128)(2,1)S(1)}, bf16[128,512]{1,0:T(8,128)(2,1)S(1)}, u32[]{:S(2)}, u32[]{:S(2)}) %collective-permute-start.3) | collective-permute-done | bytes 131104 | tf_op jit(solution)/shard_map/ppermute | solution.py:22
  134.1 4.2 %collective-permute-start.5 = (bf16[128,512]{1,0:T(8,128)(2,1)S(1)}, bf16[128,512]{1,0:T(8,128)(2,1)S(1)}, u32[]{:S(2)}, u32[]{:S(2)}) collective-permute-start(bf16[128,512]{1,0:T(8,128)(2,1)S(1)} %fusion.56), channel_id=1, source_target_pairs={{0,16},{4,20},{8,24},{12,28},{16,0},{20,4},{24,8},{28,12},{32,48},... | collective-permute-start | bytes 393224 | tf_op jit(solution)/shard_map/ppermute | solution.py:22
  138.3 1.0 copy.262
  139.4 1.1 fusion.121
  144.1 2.2 collective-permute-start.4
  146.3 1.0 copy.267
  150.2 7.0 %collective-permute-start.7 = (bf16[128,512]{1,0:T(8,128)(2,1)}, bf16[128,512]{1,0:T(8,128)(2,1)}, u32[]{:S(2)}, u32[]{:S(2)}) collective-permute-start(bf16[128,512]{1,0:T(8,128)(2,1)} %bitcast.274), channel_id=1, source_target_pairs={{0,32},{4,36},{8,40},{12,44},{16,48},{20,52},{24,56},{28,60},{32,0... | collective-permute-start | bytes 393224 | tf_op jit(solution)/shard_map/ppermute | solution.py:22
  157.2 1.0 copy.271
  162.2 4.3 %collective-permute-start.6 = (bf16[128,512]{1,0:T(8,128)(2,1)S(1)}, bf16[128,512]{1,0:T(8,128)(2,1)S(1)}, u32[]{:S(2)}, u32[]{:S(2)}) collective-permute-start(bf16[128,512]{1,0:T(8,128)(2,1)S(1)} %fusion.60), channel_id=1, source_target_pairs={{0,32},{4,36},{8,40},{12,44},{16,48},{20,52},{24,56},{28,60},{32,0... | collective-permute-start | bytes 393224 | tf_op jit(solution)/shard_map/ppermute | solution.py:22
  166.8 14.2 %collective-permute-done.6 = bf16[128,512]{1,0:T(8,128)(2,1)S(1)} collective-permute-done((bf16[128,512]{1,0:T(8,128)(2,1)S(1)}, bf16[128,512]{1,0:T(8,128)(2,1)S(1)}, u32[]{:S(2)}, u32[]{:S(2)}) %collective-permute-start.6) | collective-permute-done | bytes 131104 | tf_op jit(solution)/shard_map/ppermute | solution.py:22
  181.8 1.0 copy.283
  183.8 3.8 %fusion.13 = bf16[512,4,128]{2,0,1:T(8,128)(2,1)S(1)} fusion(f32[4,128,4,128]{3,1,0,2:T(8,128)S(1)} %copy.232, f32[512,4,128]{2,0,1:T(8,128)S(1)} %bitcast.275, f32[512,4,128]{2,0,1:T(8,128)S(1)} %bitcast.276, f32[512,4]{0,1:T(4,128)S(1)} %get-tuple-element.5, f32[512,4]{0,1:T(4,128)S(1)} %get-tuple-element.10, ...), kind=kLoop, calls=%fused_computation.27 | loop fusion | flops 4456448 | bytes 3989504 | tf_op jit(solution)/shard_map/convert_element_type | solution.py:154
  187.8 4.2 %convolution_convert_fusion = bf16[512,2048]{1,0:T(8,128)(2,1)} fusion(bf16[512,512]{0,1:T(8,128)(2,1)S(1)} %bitcast.285, bf16[512,2048]{0,1:T(8,128)(2,1)} %bitcast.79), kind=kOutput, calls=%fused_computation | convolution fusion | flops 1074790400 | bytes 4718592 | tf_op jit(solution)/shard_map/dot_general | solution.py:156
  192.0 38.4 %reduce-scatter.2.cloned.1.call-done = bf16[512,512]{1,0:T(8,128)(2,1)} async-done(((bf16[512,2048]{1,0:T(8,128)(2,1)}), bf16[512,512]{1,0:T(8,128)(2,1)}) %reduce-scatter.2.cloned.1.call-update) | async-done | bytes 524304 | tf_op jit(solution)/shard_map/reduce_scatter | solution.py:160
  (189 shorter events, 40.8 us)
Async XLA Ops:
  9.1 9.7 %copy-start.1 = (bf16[512,512]{1,0:T(8,128)(2,1)S(1)}, bf16[512,512]{1,0:T(8,128)(2,1)}, u32[]{:S(2)}) copy-start(bf16[512,512]{1,0:T(8,128)(2,1)} %param.6) | copy-start | bytes 1572868
  10.0 48.5 %collective-permute-start = (bf16[128,512]{1,0:T(8,128)(2,1)S(1)}, bf16[128,512]{1,0:T(8,128)(2,1)}, u32[]{:S(2)}, u32[]{:S(2)}) collective-permute-start(bf16[128,512]{1,0:T(8,128)(2,1)S(1)} %fusion.57), channel_id=1, source_target_pairs={{0,4},{4,0},{8,12},{12,8},{16,20},{20,16},{24,28},{28,24},{32,36},... | collective-permute-start | bytes 393224 | tf_op jit(solution)/shard_map/ppermute | solution.py:22
  21.8 39.9 %collective-permute-start.1 = (bf16[128,512]{1,0:T(8,128)(2,1)}, bf16[128,512]{1,0:T(8,128)(2,1)}, u32[]{:S(2)}, u32[]{:S(2)}) collective-permute-start(bf16[128,512]{1,0:T(8,128)(2,1)} %fusion.54), channel_id=1, source_target_pairs={{0,4},{4,0},{8,12},{12,8},{16,20},{20,16},{24,28},{28,24},{32,36},... | collective-permute-start | bytes 393224 | tf_op jit(solution)/shard_map/ppermute | solution.py:22
  25.3 15.1 %copy-start = (bf16[512,512]{1,0:T(8,128)(2,1)S(1)}, bf16[512,512]{1,0:T(8,128)(2,1)}, u32[]{:S(2)}) copy-start(bf16[512,512]{1,0:T(8,128)(2,1)} %param.5) | copy-start | bytes 1572868
  25.3 162.5 %all-to-all-start = ((bf16[128,512,16]{1,2,0:T(8,128)(2,1)}), bf16[128,512,16]{1,2,0:T(8,128)(2,1)}, u32[]{:S(2)}, u32[]{:S(2)}) async-start(bf16[128,512,16]{1,2,0:T(8,128)(2,1)} %stack.2), calls=%async_computation | async-start | bytes 4194304 | tf_op jit(solution)/shard_map/all_to_all | solution.py:14
  40.1 190.3 %reduce-scatter.2.cloned.1.call-start = ((), (), s32[]{:S(2)}) async-start(), calls=%async_computation.2 | async-start | bytes 2621440 | tf_op jit(solution)/shard_map/reduce_scatter | solution.py:160
  65.6 67.7 %collective-permute-start.3 = (bf16[128,512]{1,0:T(8,128)(2,1)S(1)}, bf16[128,512]{1,0:T(8,128)(2,1)S(1)}, u32[]{:S(2)}, u32[]{:S(2)}) collective-permute-start(bf16[128,512]{1,0:T(8,128)(2,1)S(1)} %fusion.55), channel_id=1, source_target_pairs={{0,8},{4,12},{8,0},{12,4},{16,24},{20,28},{24,16},{28,20},{32,40},... | collective-permute-start | bytes 393224 | tf_op jit(solution)/shard_map/ppermute | solution.py:22
  70.6 67.8 %collective-permute-start.2 = (bf16[128,512]{1,0:T(8,128)(2,1)S(1)}, bf16[128,512]{1,0:T(8,128)(2,1)}, u32[]{:S(2)}, u32[]{:S(2)}) collective-permute-start(bf16[128,512]{1,0:T(8,128)(2,1)S(1)} %fusion.58), channel_id=1, source_target_pairs={{0,8},{4,12},{8,0},{12,4},{16,24},{20,28},{24,16},{28,20},{32,40},... | collective-permute-start | bytes 393224 | tf_op jit(solution)/shard_map/ppermute | solution.py:22
  134.1 14.1 %collective-permute-start.5 = (bf16[128,512]{1,0:T(8,128)(2,1)S(1)}, bf16[128,512]{1,0:T(8,128)(2,1)S(1)}, u32[]{:S(2)}, u32[]{:S(2)}) collective-permute-start(bf16[128,512]{1,0:T(8,128)(2,1)S(1)} %fusion.56), channel_id=1, source_target_pairs={{0,16},{4,20},{8,24},{12,28},{16,0},{20,4},{24,8},{28,12},{32,48},... | collective-permute-start | bytes 393224 | tf_op jit(solution)/shard_map/ppermute | solution.py:22
  144.1 13.1 %collective-permute-start.4 = (bf16[128,512]{1,0:T(8,128)(2,1)}, bf16[128,512]{1,0:T(8,128)(2,1)}, u32[]{:S(2)}, u32[]{:S(2)}) collective-permute-start(bf16[128,512]{1,0:T(8,128)(2,1)} %fusion.59), channel_id=1, source_target_pairs={{0,16},{4,20},{8,24},{12,28},{16,0},{20,4},{24,8},{28,12},{32,48},... | collective-permute-start | bytes 393224 | tf_op jit(solution)/shard_map/ppermute | solution.py:22
  147.4 10.9 %copy-start.14 = (bf16[32,512]{1,0:T(8,128)(2,1)S(1)}, bf16[32,512]{1,0:T(8,128)(2,1)}, u32[]{:S(2)}) copy-start(bf16[32,512]{1,0:T(8,128)(2,1)} %get-tuple-element.16) | copy-start | bytes 98308
  150.2 31.7 %collective-permute-start.7 = (bf16[128,512]{1,0:T(8,128)(2,1)}, bf16[128,512]{1,0:T(8,128)(2,1)}, u32[]{:S(2)}, u32[]{:S(2)}) collective-permute-start(bf16[128,512]{1,0:T(8,128)(2,1)} %bitcast.274), channel_id=1, source_target_pairs={{0,32},{4,36},{8,40},{12,44},{16,48},{20,52},{24,56},{28,60},{32,0... | collective-permute-start | bytes 393224 | tf_op jit(solution)/shard_map/ppermute | solution.py:22
  159.4 7.0 %copy-start.9 = (bf16[128,512]{1,0:T(8,128)(2,1)S(1)}, bf16[128,512]{1,0:T(8,128)(2,1)}, u32[]{:S(2)}) copy-start(bf16[128,512]{1,0:T(8,128)(2,1)} %copy-done.8) | copy-start | bytes 393220
  161.2 5.3 %copy-start.19 = (f32[4,32]{1,0:T(4,128)S(1)}, f32[4,32]{1,0:T(4,128)}, u32[]{:S(2)}) copy-start(f32[4,32]{1,0:T(4,128)} %copy-done.18) | copy-start | bytes 1540
  161.2 19.9 %copy-start.16 = (bf16[16,512]{1,0:T(8,128)(2,1)S(1)}, bf16[16,512]{1,0:T(8,128)(2,1)}, u32[]{:S(2)}) copy-start(bf16[16,512]{1,0:T(8,128)(2,1)} %convert_reduce_fusion.4) | copy-start | bytes 49156
  161.3 21.8 %copy-start.17 = (f32[4,4,128]{2,1,0:T(4,128)S(1)}, f32[4,4,128]{2,1,0:T(4,128)}, u32[]{:S(2)}) copy-start(f32[4,4,128]{2,1,0:T(4,128)} %fusion.1) | copy-start | bytes 24580
  161.6 21.5 %copy-start.20 = (f32[512,4]{0,1:T(4,128)S(1)}, f32[512,4]{0,1:T(4,128)}, u32[]{:S(2)}) copy-start(f32[512,4]{0,1:T(4,128)} %copy.286) | copy-start | bytes 24580
  161.6 21.5 %copy-start.21 = (f32[512,4]{0,1:T(4,128)S(1)}, f32[512,4]{0,1:T(4,128)}, u32[]{:S(2)}) copy-start(f32[512,4]{0,1:T(4,128)} %reshape.862) | copy-start | bytes 24580
  161.7 21.5 %copy-start.22 = (f32[512,4]{0,1:T(4,128)S(1)}, f32[512,4]{0,1:T(4,128)}, u32[]{:S(2)}) copy-start(f32[512,4]{0,1:T(4,128)} %reshape.864) | copy-start | bytes 24580
  161.7 21.5 %copy-start.23 = (f32[512,4]{0,1:T(4,128)S(1)}, f32[512,4]{0,1:T(4,128)}, u32[]{:S(2)}) copy-start(f32[512,4]{0,1:T(4,128)} %reshape.848) | copy-start | bytes 24580
  161.7 21.5 %copy-start.24 = (f32[512,4]{0,1:T(4,128)S(1)}, f32[512,4]{0,1:T(4,128)}, u32[]{:S(2)}) copy-start(f32[512,4]{0,1:T(4,128)} %reshape.866) | copy-start | bytes 24580
  161.7 21.5 %copy-start.25 = (f32[512,4]{0,1:T(4,128)S(1)}, f32[512,4]{0,1:T(4,128)}, u32[]{:S(2)}) copy-start(f32[512,4]{0,1:T(4,128)} %get-tuple-element.18) | copy-start | bytes 24580
  161.7 21.5 %copy-start.26 = (f32[512,4]{0,1:T(4,128)S(1)}, f32[512,4]{0,1:T(4,128)}, u32[]{:S(2)}) copy-start(f32[512,4]{0,1:T(4,128)} %get-tuple-element.19) | copy-start | bytes 24580
  162.2 18.8 %collective-permute-start.6 = (bf16[128,512]{1,0:T(8,128)(2,1)S(1)}, bf16[128,512]{1,0:T(8,128)(2,1)S(1)}, u32[]{:S(2)}, u32[]{:S(2)}) collective-permute-start(bf16[128,512]{1,0:T(8,128)(2,1)S(1)} %fusion.60), channel_id=1, source_target_pairs={{0,32},{4,36},{8,40},{12,44},{16,48},{20,52},{24,56},{28,60},{32,0... | collective-permute-start | bytes 393224 | tf_op jit(solution)/shard_map/ppermute | solution.py:22
  (14 other events, 33.3 us)
Sparse Core Ops, SparseCore 0:
  192.1 38.2 reduce-scatter.1
